TPU v7x, 256 devices: a whole 4x4x8 slice. The times are simulated.
256 devices in a mesh: dp: 32 (over y, x, core), tensor: 8 (over z).
Axes of the slice: x: 4, y: 4, z: 8, core: 2. Of those that a mesh axis runs over, the one named last changes fastest.
Arguments:
- patches: bfloat16 [16384, 1280], P('dp'), may hold values from -6 to 6
- window_ids: int32 [32, 512], P('dp'), may hold values from 0 to 15, never falling along the last dimension, each value on 1 to 64 neighbouring positions
- vit_gain: float32 [1280], replicated, may hold values from 0.5 to 2
- qkv_weight: bfloat16 [3, 1280, 1280], P(None, None, 'tensor'), may hold values from -0.15625 to 0.15625
- out_weight: bfloat16 [1280, 1280], P('tensor'), may hold values from -0.15625 to 0.15625
- merge_gain: float32 [1280], replicated, may hold values from 0.5 to 2
- merger_weight: bfloat16 [5120, 3584], P(None, 'tensor'), may hold values from -0.078125 to 0.078125
- audio: bfloat16 [12288, 3584], P('dp', 'tensor'), may hold values from -6 to 6
- span_lengths: int32 [32, 32], replicated, may hold values from 8 to 32, as said below
- span_time: int32 [32, 32], replicated, may hold values from 0 to 31, each once within a row
- llm_gain: float32 [3584], replicated, may hold values from 0.5 to 2
- gate_weight: bfloat16 [3584, 9472], P('dp', 'tensor'), may hold values from -0.09375 to 0.09375
- up_weight: bfloat16 [3584, 9472], P('dp', 'tensor'), may hold values from -0.09375 to 0.09375
- down_weight: bfloat16 [9472, 3584], P('tensor', 'dp'), may hold values from -0.0625 to 0.0625
Outputs:
- mixed: bfloat16 [16384, 3584], P(('dp', 'tensor'))
Inputs may be any that keep to these rules, and one draw needn't show every extreme that they name: `span_lengths`: every row and every column sums to 512; every row and every column holds the value 32 at least once. `span_time`: each row is a permutation of the owners' numbers. `window_ids`: window numbers never fall along a row; a window holds at most 64 patches.
All inputs are finite; a program needn't handle non-finite values.
Results may differ from a plain program's by a relative error of at most 0.017.
Values may be sent and summed in bfloat16 or wider, within the bound.
No kernel may reach another device: no remote copies, remote signals or barrier semaphores. Data moves between devices by JAX's collectives and lax.ppermute only.
A program may use at most 128 MiB of HBM per device.

v0:
```python
import math
import jax
import jax.numpy as jnp
from jax import lax
from jax.sharding import PartitionSpec as P

D_VIT = 1280
HEAD_VIT = 80
EPSILON = 1e-06


def in_blocks(x, dim, devices):
    before, after = (x.shape[:dim], x.shape[dim + 1 :])
    return jnp.moveaxis(x.reshape(*before, devices, -1, *after), dim, 0)


def sent_and_summed(x, axis, dim):
    parts = in_blocks(x, dim, lax.axis_size(axis))
    arrived = lax.all_to_all(parts, axis, split_axis=0, concat_axis=0, tiled=True)
    return arrived.astype(jnp.float32).sum(axis=0)


def from_everyone(x, axis):
    devices = lax.axis_size(axis)
    return lax.all_to_all(jnp.broadcast_to(x[None], (devices, *x.shape)), axis, 0, 0, tiled=True)


def in_order(parts, dim):
    parts = jnp.moveaxis(parts, 0, dim)
    dims = parts.shape
    return parts.reshape(*dims[:dim], dims[dim] * dims[dim + 1], *dims[dim + 2 :])


def gather_directly(x, axis, dim):
    parts = from_everyone(x, axis)
    return in_order(parts, dim)


def gather_turned(arrays, axis, dims):
    turned = [jnp.moveaxis(a, dim, 0) for a, dim in zip(arrays, dims)]
    widths = [t[0].size for t in turned]
    both = jnp.concatenate([t.reshape(-1, w) for t, w in zip(turned, widths)], axis=1)
    whole = lax.all_gather(both, axis, axis=0, tiled=True)
    parts = jnp.split(whole, [sum(widths[:k]) for k in range(1, len(widths))], axis=1)
    return tuple(
        (
            jnp.moveaxis(b.reshape(-1, *t.shape[1:]), 0, dim)
            for b, t, dim in zip(parts, turned, dims)
        )
    )


def rms_scale(values, gain):
    wide = values.astype(jnp.float32)
    meansq = jnp.mean(wide * wide, axis=-1, keepdims=True)
    return wide * lax.rsqrt(meansq + EPSILON) * gain


def body(
    patches,
    window_ids,
    vit_gain,
    qkv_weight,
    out_weight,
    merge_gain,
    merger_weight,
    audio,
    span_lengths,
    span_time,
    llm_gain,
    gate_weight,
    up_weight,
    down_weight,
):
    patch_count = patches.shape[0]
    heads_here = qkv_weight.shape[2] // HEAD_VIT
    normed = rms_scale(patches, vit_gain).astype(jnp.bfloat16)
    query = jnp.dot(normed, qkv_weight[0], preferred_element_type=jnp.float32).astype(jnp.bfloat16)
    keys = jnp.dot(normed, qkv_weight[1], preferred_element_type=jnp.float32).astype(jnp.bfloat16)
    values = jnp.dot(normed, qkv_weight[2], preferred_element_type=jnp.float32).astype(jnp.bfloat16)
    query = query.reshape(patch_count, heads_here, HEAD_VIT)
    keys = keys.reshape(patch_count, heads_here, HEAD_VIT)
    values = values.reshape(patch_count, heads_here, HEAD_VIT)
    scores = jnp.einsum(
        "phe,qhe->hpq", query, keys, preferred_element_type=jnp.float32
    ) / math.sqrt(HEAD_VIT)
    windows = window_ids[0]
    same = windows[:, None] == windows[None, :]
    scores = jnp.where(same[None], scores, -1e30)
    probs = jax.nn.softmax(scores, axis=-1).astype(jnp.bfloat16)
    context = jnp.einsum("hpq,qhe->phe", probs, values, preferred_element_type=jnp.float32).astype(
        jnp.bfloat16
    )
    context = context.reshape(patch_count, heads_here * HEAD_VIT)
    partial_value = jnp.dot(context, out_weight, preferred_element_type=jnp.float32)
    share = sent_and_summed(partial_value.astype(jnp.bfloat16), "tensor", 0)
    share_rows = share.shape[0]
    own_frames = lax.dynamic_slice_in_dim(
        patches, lax.axis_index("tensor") * share_rows, share_rows, 0
    )
    own_encoded = (own_frames.astype(jnp.float32) + share).astype(jnp.bfloat16)
    encoded = gather_directly(own_encoded, "tensor", 0)
    merged = (
        rms_scale(encoded, merge_gain).astype(jnp.bfloat16).reshape(patch_count // 4, 4 * D_VIT)
    )
    video = jnp.dot(merged, merger_weight, preferred_element_type=jnp.float32).astype(jnp.bfloat16)
    source = jnp.concatenate([video, audio], axis=0)
    seq_count = source.shape[0]
    owner_count = lax.axis_size("dp")
    owner = lax.axis_index("dp")
    capacity = 2 * seq_count // owner_count
    sent_lengths = span_lengths[owner]
    starts = jnp.cumsum(sent_lengths) - sent_lengths
    slot_index = jnp.arange(capacity, dtype=jnp.int32)
    occupied = slot_index[None, :] < sent_lengths[:, None]
    source_index = jnp.where(occupied, starts[:, None] + slot_index[None, :], 0).reshape(-1)
    outgoing = jnp.take(source, source_index, axis=0)
    outgoing = jnp.where(occupied.reshape(-1)[:, None], outgoing, jnp.zeros((), outgoing.dtype))
    incoming = lax.all_to_all(outgoing, "dp", split_axis=0, concat_axis=0, tiled=True)
    taken_lengths = span_lengths[:, owner]
    arrival = span_time[owner]
    earlier = arrival[:, None] < arrival[None, :]
    offsets = jnp.sum(jnp.where(earlier, taken_lengths[:, None], 0), axis=0)
    position = jnp.arange(seq_count, dtype=jnp.int32)
    inside = (position[None, :] >= offsets[:, None]) & (
        position[None, :] < offsets[:, None] + taken_lengths[:, None]
    )
    sender = jnp.arange(owner_count, dtype=jnp.int32)[:, None]
    slot_row = sender * capacity + position[None, :] - offsets[:, None]
    picked = jnp.sum(jnp.where(inside, slot_row, 0), axis=0)
    sequence = jnp.take(incoming, picked, axis=0)
    features = lax.all_gather(sequence, "tensor", axis=1, tiled=True)
    normed_seq = rms_scale(features, llm_gain).astype(jnp.bfloat16)
    gate_full, up_full, down_full = gather_turned(
        (gate_weight, up_weight, down_weight), "dp", (0, 0, 1)
    )
    gate = jnp.dot(normed_seq, gate_full, preferred_element_type=jnp.float32)
    upward = jnp.dot(normed_seq, up_full, preferred_element_type=jnp.float32)
    hidden = (jax.nn.silu(gate) * upward).astype(jnp.bfloat16)
    terms = jnp.dot(hidden, down_full, preferred_element_type=jnp.float32)
    summed = lax.psum_scatter(
        terms.astype(jnp.bfloat16), "tensor", scatter_dimension=0, tiled=True
    ).astype(jnp.float32)
    own_count = summed.shape[0]
    own_rows = lax.dynamic_slice_in_dim(
        features, lax.axis_index("tensor") * own_count, own_count, 0
    )
    return (own_rows.astype(jnp.float32) + summed).astype(jnp.bfloat16)


def solution(mesh):
    return jax.shard_map(
        body,
        mesh=mesh,
        in_specs=(
            P("dp", None),
            P("dp", None),
            P(),
            P(None, None, "tensor"),
            P("tensor", None),
            P(),
            P(None, "tensor"),
            P("dp", "tensor"),
            P(),
            P(),
            P(),
            P("dp", "tensor"),
            P("dp", "tensor"),
            P("tensor", "dp"),
        ),
        out_specs=P(("dp", "tensor"), None),
        check_vma=False,
    )
```

profile of v0, /device:TPU:1, one launch (start us, length us, event | category | flops | bytes accessed | tf_op | source)
XLA Modules:
  0.0 377.8 jit_solution(1047735685525039576)
XLA Ops:
  6.5 1.8 fusion.19
  8.4 2.1 convolution_convert_fusion.3
  14.3 1.6 convolution_convert_fusion
  15.9 9.0 %all-to-all-start = ((bf16[8,64,1280]{2,1,0:T(8,128)(2,1)}), bf16[8,64,1280]{2,1,0:T(8,128)(2,1)S(1)}, u32[]{:S(2)}, u32[]{:S(2)}) async-start(bf16[8,64,1280]{2,1,0:T(8,128)(2,1)} %bitcast.15), calls=%async_computation | async-start | bytes 2621440 | tf_op jit(solution)/shard_map/all_to_all | solution.py:19
  24.9 34.9 %all-to-all-done = bf16[8,64,1280]{2,1,0:T(8,128)(2,1)S(1)} async-done(((bf16[8,64,1280]{2,1,0:T(8,128)(2,1)}), bf16[8,64,1280]{2,1,0:T(8,128)(2,1)S(1)}, u32[]{:S(2)}, u32[]{:S(2)}) %all-to-all-start) | async-done | bytes 1310752 | tf_op jit(solution)/shard_map/all_to_all | solution.py:19
  61.2 3.6 all-to-all-start.1
  66.6 32.9 %all-to-all-done.1 = bf16[8,64,1280]{2,1,0:T(8,128)(2,1)S(1)} async-done(((bf16[8,64,1280]{2,1,0:T(8,128)(2,1)}), bf16[8,64,1280]{2,1,0:T(8,128)(2,1)S(1)}, u32[]{:S(2)}, u32[]{:S(2)}) %all-to-all-start.1) | async-done | bytes 1310752 | tf_op jit(solution)/shard_map/all_to_all | solution.py:25
  100.4 2.0 copy.42
  102.3 1.9 reshape.242
  104.2 5.2 %fusion.25 = bf16[128,448]{0,1:T(8,128)(2,1)S(1)} fusion(bf16[5120,448]{0,1:T(8,128)(2,1)} %param.20, f32[128,5120]{1,0:T(8,128)} %reshape.242, f32[128,5120]{1,0:T(8,128)} %bitcast.49, f32[5120]{0:T(1024)S(1)} %mul.101), kind=kOutput, calls=%fused_computation.36 | convolution fusion | flops 589225984 | bytes 9965568 | tf_op jit(solution)/shard_map/dot_general | solution.py:106
  109.6 4.0 %gather_fusion = bf16[1024,448]{1,0:T(8,128)(2,1)S(1)} fusion(bf16[512,448]{1,0:T(8,128)(2,1)S(1)} %pad_maximum_fusion, s32[1024]{0:T(1024)S(1)} %broadcast_clamp_fusion), kind=kCustom, calls=%fused_computation | custom fusion | bytes 1839104 | tf_op jit(solution)/shard_map/jit(_take)/gather | solution.py:117
  113.6 1.3 select_select_fusion
  114.9 7.6 %all-to-all-start.2 = ((bf16[32,32,448]{2,1,0:T(8,128)(2,1)}), bf16[32,32,448]{2,1,0:T(8,128)(2,1)S(1)}, u32[]{:S(2)}, u32[]{:S(2)}) async-start(bf16[32,32,448]{2,1,0:T(8,128)(2,1)} %select_select_fusion), calls=%async_computation.2 | async-start | bytes 2097152 | tf_op jit(solution)/shard_map/all_to_all | solution.py:119
  122.6 17.0 %all-to-all-done.2 = bf16[32,32,448]{2,1,0:T(8,128)(2,1)S(1)} async-done(((bf16[32,32,448]{2,1,0:T(8,128)(2,1)}), bf16[32,32,448]{2,1,0:T(8,128)(2,1)S(1)}, u32[]{:S(2)}, u32[]{:S(2)}) %all-to-all-start.2) | async-done | bytes 917536 | tf_op jit(solution)/shard_map/all_to_all | solution.py:119
  139.6 2.0 gather_fusion.1
  142.8 1.4 concatenate.7
  144.4 40.7 %all-gather.3.cloned.1.call-done = bf16[512,3584]{0,1:T(8,128)(2,1)} async-done(((bf16[512,448]{0,1:T(8,128)(2,1)}), bf16[512,3584]{0,1:T(8,128)(2,1)}) %all-gather.3.cloned.1.call-update) | async-done | bytes 3670032 | tf_op jit(solution)/shard_map/all_gather | solution.py:132
  185.1 2.9 fusion.7
  188.0 97.1 %all-gather.5.cloned.1.call-done = bf16[3584,3552]{1,0:T(8,128)(2,1)} async-done(((bf16[112,3552]{1,0:T(8,128)(2,1)}), bf16[3584,3552]{1,0:T(8,128)(2,1)}) %all-gather.5.cloned.1.call-update) | async-done | bytes 25460752 | tf_op jit(solution)/shard_map/all_gather | solution.py:43
  285.1 9.8 %fusion.5 = f32[512,1184]{0,1:T(8,128)S(1)} fusion(bf16[3584,3552]{1,0:T(8,128)(2,1)} %all-gather.5.cloned.1.call-done, bf16[512,3584]{0,1:T(8,128)(2,1)} %all-gather.3.cloned.1.call-done, f32[3584]{0:T(1024)S(1)} %copy-done.11, f32[512]{0:T(512)S(1)} %add_rsqrt_fusion.1), kind=kOutput, calls=%fused_computation.7 | convolution fusion | flops 4352638976 | bytes 15286272 | tf_op jit(solution)/shard_map/dot_general | solution.py:137
  294.9 24.9 %fusion.10 = bf16[512,3584]{1,0:T(8,128)(2,1)} fusion(bf16[3584,3552]{1,0:T(8,128)(2,1)} %all-gather.5.cloned.1.call-done, f32[512,1184]{0,1:T(8,128)S(1)} %fusion.5, bf16[512,3584]{0,1:T(8,128)(2,1)} %all-gather.3.cloned.1.call-done, f32[3584]{0:T(1024)S(1)} %copy-done.11, f32[512]{0:T(512)S(1)} %add_rsqrt_fusion.1), kind=kOutput, calls=%fused_computation.14 | convolution fusion | flops 8703410176 | bytes 28131328 | tf_op jit(solution)/shard_map/dot_general | solution.py:140
  319.8 1.6 constant_dynamic-slice_fusion
  321.7 47.7 %reduce-scatter.2.cloned.1.call-done = bf16[64,3584]{1,0:T(8,128)(2,1)} async-done(((bf16[512,3584]{1,0:T(8,128)(2,1)}), bf16[64,3584]{1,0:T(8,128)(2,1)}) %reduce-scatter.2.cloned.1.call-update) | async-done | bytes 458768 | tf_op jit(solution)/shard_map/reduce_scatter | solution.py:141
  369.4 1.9 add_convert_fusion
  (74 shorter events, 9.8 us)
Async XLA Ops:
  6.5 7.7 %copy-start = (bf16[160,1280]{1,0:T(8,128)(2,1)S(1)}, bf16[160,1280]{1,0:T(8,128)(2,1)}, u32[]{:S(2)}) copy-start(bf16[160,1280]{1,0:T(8,128)(2,1)} %param.18) | copy-start | bytes 1228804
  6.5 3.9 %copy-start.2 = (bf16[512,1280]{1,0:T(8,128)(2,1)S(1)}, bf16[512,1280]{1,0:T(8,128)(2,1)}, u32[]{:S(2)}) copy-start(bf16[512,1280]{1,0:T(8,128)(2,1)} %param.14) | copy-start | bytes 3932164
  6.5 3.9 %copy-start.12 = (f32[1280]{0:T(1024)S(1)}, f32[1280]{0:T(1024)}, u32[]{:S(2)}) copy-start(f32[1280]{0:T(1024)} %param.16) | copy-start | bytes 15364
  6.5 3.9 %copy-start.10 = (bf16[3,1280,160]{1,2,0:T(8,128)(2,1)S(1)}, bf16[3,1280,160]{1,2,0:T(8,128)(2,1)}, u32[]{:S(2)}) copy-start(bf16[3,1280,160]{1,2,0:T(8,128)(2,1)} %param.17) | copy-start | bytes 3686404
  10.5 1.3 copy-start.8
  15.9 43.9 %all-to-all-start = ((bf16[8,64,1280]{2,1,0:T(8,128)(2,1)}), bf16[8,64,1280]{2,1,0:T(8,128)(2,1)S(1)}, u32[]{:S(2)}, u32[]{:S(2)}) async-start(bf16[8,64,1280]{2,1,0:T(8,128)(2,1)} %bitcast.15), calls=%async_computation | async-start | bytes 2621440 | tf_op jit(solution)/shard_map/all_to_all | solution.py:19
  60.0 4.8 %copy-start.9 = (f32[1280]{0:T(1024)S(1)}, f32[1280]{0:T(1024)}, u32[]{:S(2)}) copy-start(f32[1280]{0:T(1024)} %param.19) | copy-start | bytes 15364
  60.0 4.8 %copy-start.3 = (bf16[384,448]{0,1:T(8,128)(2,1)S(1)}, bf16[384,448]{0,1:T(8,128)(2,1)}, u32[]{:S(2)}) copy-start(bf16[384,448]{0,1:T(8,128)(2,1)} %param.21) | copy-start | bytes 1032196
  60.0 5.0 %copy-start.7 = (s32[32,32]{1,0:T(8,128)S(1)}, s32[32,32]{1,0:T(8,128)}, u32[]{:S(2)}) copy-start(s32[32,32]{1,0:T(8,128)} %param.22) | copy-start | bytes 12292
  61.2 38.3 %all-to-all-start.1 = ((bf16[8,64,1280]{2,1,0:T(8,128)(2,1)}), bf16[8,64,1280]{2,1,0:T(8,128)(2,1)S(1)}, u32[]{:S(2)}, u32[]{:S(2)}) async-start(bf16[8,64,1280]{2,1,0:T(8,128)(2,1)} %broadcast_in_dim.103), calls=%async_computation.1 | async-start | bytes 2621440 | tf_op jit(solution)/shard_map/all_to_all | solution.py:25
  114.9 24.8 %all-to-all-start.2 = ((bf16[32,32,448]{2,1,0:T(8,128)(2,1)}), bf16[32,32,448]{2,1,0:T(8,128)(2,1)S(1)}, u32[]{:S(2)}, u32[]{:S(2)}) async-start(bf16[32,32,448]{2,1,0:T(8,128)(2,1)} %select_select_fusion), calls=%async_computation.2 | async-start | bytes 2097152 | tf_op jit(solution)/shard_map/all_to_all | solution.py:119
  122.4 62.7 %all-gather.3.cloned.1.call-start = ((), (), s32[]{:S(2)}) async-start(), calls=%async_computation.4 | async-start | bytes 4128768 | tf_op jit(solution)/shard_map/all_gather | solution.py:132
  139.6 3.2 copy-start.4
  139.6 3.2 copy-start.5
  139.6 3.2 copy-start.6
  142.7 142.4 %all-gather.5.cloned.1.call-start = ((), (), s32[]{:S(2)}) async-start(), calls=%async_computation.5 | async-start | bytes 26492928 | tf_op jit(solution)/shard_map/all_gather | solution.py:43
  144.1 141.0 %copy-start.11 = (f32[3584]{0:T(1024)S(1)}, f32[3584]{0:T(1024)}, u32[]{:S(2)}) copy-start(f32[3584]{0:T(1024)} %param.24) | copy-start | bytes 43012
  144.2 225.2 %reduce-scatter.2.cloned.1.call-start = ((), (), s32[]{:S(2)}) async-start(), calls=%async_computation.6 | async-start | bytes 4128768 | tf_op jit(solution)/shard_map/reduce_scatter | solution.py:141
  319.8 51.5 %copy-start.1 = (bf16[160,1280]{1,0:T(8,128)(2,1)S(1)}, bf16[160,1280]{1,0:T(8,128)(2,1)}, u32[]{:S(2)}) copy-start(bf16[160,1280]{1,0:T(8,128)(2,1)} %param.18) | copy-start | bytes 1228804
Sparse Core Ops, SparseCore 0:
  142.8 42.2 all-gather.2
  187.7 97.3 all-gather.4
  319.9 49.4 reduce-scatter.1
where the time goes:
time: 378 us
  waiting for transfers between devices  270 us (71%)
  matrix products  47.1 us (12%)
  starting transfers between devices  20.5 us (5%)
  local copies, waits for them, and re-layouts  17 us (4%)
  between operations  13.5 us (4%)
  other arithmetic  9.35 us (2%)
    all_gather x1, waiting for transfers between devices, gather_turned(): whole = lax.all_gather(both, axis, axis=0, tiled=True)  97.1 us
    reduce_scatter x1, waiting for transfers between devices, body(): lax.psum_scatter(terms.astype(jnp.bfloat16), 'tensor', scatter_dimension=...  47.7 us
    all_gather x1, waiting for transfers between devices, body(): features = lax.all_gather(sequence, 'tensor', axis=1, tiled=True)  40.7 us
    all_to_all x1, waiting for transfers between devices, sent_and_summed(): lax.all_to_all(parts, axis, split_axis=0, concat_axis=0, tiled=True)  34.9 us
    all_to_all x1, waiting for transfers between devices, from_everyone(): lax.all_to_all(jnp.broadcast_to(x[None], (devices, *x.shape)), axis, 0, 0...  32.9 us
    dot_general x1, matrix products, body(): terms = jnp.dot(hidden, down_full, preferred_element_type=jnp.float32)  24.9 us
    all_to_all x1, waiting for transfers between devices, body(): lax.all_to_all(outgoing, 'dp', split_axis=0, concat_axis=0, tiled=True)  17 us
    dot_general x1, matrix products, body(): gate = jnp.dot(normed_seq, gate_full, preferred_element_type=jnp.float32)  9.77 us
  transfers between devices with their start and end apart: 6, of which 6 were waited for; matrix products, arithmetic and copies ran while one was open for 2% of the time, Pallas kernels for 0%

commit v1 on v0

--- a/solution.py
+++ b/solution.py
@@ -7,6 +7,19 @@
 D_VIT = 1280
 HEAD_VIT = 80
 EPSILON = 1e-06
+
+
+def ring_gather(x, axis, dim):
+    ways = lax.axis_size(axis)
+    up = [(d, (d + 1) % ways) for d in range(ways)]
+    down = [(d, (d - 1) % ways) for d in range(ways)]
+    earlier, later = ([x], [x])
+    for _ in range(ways // 2):
+        earlier.append(lax.ppermute(earlier[-1], axis, up))
+    for _ in range((ways - 1) // 2):
+        later.append(lax.ppermute(later[-1], axis, down))
+    line = jnp.concatenate([*earlier[::-1], *later[1:]], axis=dim)
+    return jnp.roll(line, (lax.axis_index(axis) - ways // 2) * x.shape[dim], axis=dim)
 
 
 def in_blocks(x, dim, devices):
@@ -129,7 +142,7 @@
     slot_row = sender * capacity + position[None, :] - offsets[:, None]
     picked = jnp.sum(jnp.where(inside, slot_row, 0), axis=0)
     sequence = jnp.take(incoming, picked, axis=0)
-    features = lax.all_gather(sequence, "tensor", axis=1, tiled=True)
+    features = ring_gather(sequence, "tensor", 1)
     normed_seq = rms_scale(features, llm_gain).astype(jnp.bfloat16)
     gate_full, up_full, down_full = gather_turned(
         (gate_weight, up_weight, down_weight), "dp", (0, 0, 1)

time: 378 us -> 314 us (0.83)
  waiting for transfers between devices: 270 us -> 178 us
  local copies, waits for them, and re-layouts: 17 us -> 27 us
  starting transfers between devices: 20.5 us -> 28.6 us
  matrix products: 47.1 us -> 54.4 us
    all_gather x1, waiting for transfers between devices: 97.1 us -> 0.02 us  [gather_turned(): whole = lax.all_gather(both, axis, axis=0, tiled=True)]
    ppermute x0 -> x7, waiting for transfers between devices: none -> 43.8 us  [the longest x4 43.8 us: ring_gather(): earlier.append(lax.ppermute(earlier[-1], axis, up))]
    all_gather x1 -> x0, waiting for transfers between devices: 40.7 us -> none  [body(): features = lax.all_gather(sequence, 'tensor', axis=1, tiled=True)]
    dot_general x0 -> x1, matrix products: none -> 14.2 us  [body(): upward = jnp.dot(normed_seq, up_full, preferred_element_type=jnp.float32)]
    concatenate x0 -> x1, local copies, waits for them, and re-layouts: none -> 11.6 us  [ring_gather(): jnp.roll(line, (lax.axis_index(axis) - ways // 2) * x.shape[dim], axis=dim)]
    dot_general x1, matrix products: 24.9 us -> 15.8 us  [body(): terms = jnp.dot(hidden, down_full, preferred_element_type=jnp.float32)]
    ppermute x0 -> x7, starting transfers between devices: none -> 8.11 us  [the longest x3 7.73 us: ring_gather(): later.append(lax.ppermute(later[-1], axis, down))]
  transfers between devices with their start and end apart: 6 -> 12, of which waited for: 6 -> 8; matrix products, arithmetic and copies ran while one was open for 2% -> 15% of each run, Pallas kernels for 0% -> 0%
where the time goes in v1:
time: 314 us; the launch traced here: 312 us
  waiting for transfers between devices  178 us (57%)
  matrix products  54.4 us (17%)
  starting transfers between devices  28.6 us (9%)
  local copies, waits for them, and re-layouts  27 us (9%)
  between operations  13.8 us (4%)
  other arithmetic  10.5 us (3%)
    reduce_scatter x1, waiting for transfers between devices, body(): lax.psum_scatter(terms.astype(jnp.bfloat16), 'tensor', scatter_dimension=...  49.2 us
    ppermute x4, waiting for transfers between devices, ring_gather(): earlier.append(lax.ppermute(earlier[-1], axis, up))  43.8 us
    all_to_all x1, waiting for transfers between devices, sent_and_summed(): lax.all_to_all(parts, axis, split_axis=0, concat_axis=0, tiled=True)  34.9 us
    all_to_all x1, waiting for transfers between devices, from_everyone(): lax.all_to_all(jnp.broadcast_to(x[None], (devices, *x.shape)), axis, 0, 0...  33 us
    all_to_all x1, waiting for transfers between devices, body(): lax.all_to_all(outgoing, 'dp', split_axis=0, concat_axis=0, tiled=True)  17 us
    dot_general x1, matrix products, body(): terms = jnp.dot(hidden, down_full, preferred_element_type=jnp.float32)  15.8 us
    dot_general x1, matrix products, body(): upward = jnp.dot(normed_seq, up_full, preferred_element_type=jnp.float32)  14.2 us
    concatenate x1, local copies, waits for them, and re-layouts, ring_gather(): jnp.roll(line, (lax.axis_index(axis) - ways // 2) * x.shape[dim], axis=dim)  11.6 us
  transfers between devices with their start and end apart: 12, of which 8 were waited for; matrix products, arithmetic and copies ran while one was open for 15% of the time, Pallas kernels for 0%

profile of v1, /device:TPU:1, one launch (start us, length us, event | category | flops | bytes accessed | tf_op | source)
XLA Modules:
  0.0 312.2 jit_solution(475434443989635854)
XLA Ops:
  6.6 2.4 concatenate.14
  18.5 9.0 %all-to-all-start = ((bf16[8,64,1280]{2,1,0:T(8,128)(2,1)}), bf16[8,64,1280]{2,1,0:T(8,128)(2,1)S(1)}, u32[]{:S(2)}, u32[]{:S(2)}) async-start(bf16[8,64,1280]{2,1,0:T(8,128)(2,1)} %bitcast.15), calls=%async_computation | async-start | bytes 2621440 | tf_op jit(solution)/shard_map/all_to_all | solution.py:32
  27.5 34.9 %all-to-all-done = bf16[8,64,1280]{2,1,0:T(8,128)(2,1)S(1)} async-done(((bf16[8,64,1280]{2,1,0:T(8,128)(2,1)}), bf16[8,64,1280]{2,1,0:T(8,128)(2,1)S(1)}, u32[]{:S(2)}, u32[]{:S(2)}) %all-to-all-start) | async-done | bytes 1310752 | tf_op jit(solution)/shard_map/all_to_all | solution.py:32
  63.9 3.6 %all-to-all-start.1 = ((bf16[8,64,1280]{2,1,0:T(8,128)(2,1)}), bf16[8,64,1280]{2,1,0:T(8,128)(2,1)S(1)}, u32[]{:S(2)}, u32[]{:S(2)}) async-start(bf16[8,64,1280]{2,1,0:T(8,128)(2,1)} %broadcast_in_dim.103), calls=%async_computation.1 | async-start | bytes 2621440 | tf_op jit(solution)/shard_map/all_to_all | solution.py:38
  69.2 33.0 %all-to-all-done.1 = bf16[8,64,1280]{2,1,0:T(8,128)(2,1)S(1)} async-done(((bf16[8,64,1280]{2,1,0:T(8,128)(2,1)}), bf16[8,64,1280]{2,1,0:T(8,128)(2,1)S(1)}, u32[]{:S(2)}, u32[]{:S(2)}) %all-to-all-start.1) | async-done | bytes 1310752 | tf_op jit(solution)/shard_map/all_to_all | solution.py:38
  103.0 2.0 copy.32
  107.0 5.2 %fusion.20 = bf16[128,448]{0,1:T(8,128)(2,1)S(1)} fusion(bf16[5120,448]{0,1:T(8,128)(2,1)} %param.20, f32[128,5120]{1,0:T(8,128)} %reshape.242, f32[128,5120]{1,0:T(8,128)} %bitcast.49, f32[5120]{0:T(1024)S(1)} %mul.104), kind=kOutput, calls=%fused_computation.36 | convolution fusion | flops 589225984 | bytes 9965568 | tf_op jit(solution)/shard_map/dot_general | solution.py:119
  112.4 4.0 %gather_fusion = bf16[1024,448]{1,0:T(8,128)(2,1)S(1)} fusion(bf16[512,448]{1,0:T(8,128)(2,1)S(1)} %pad_maximum_fusion, s32[1024]{0:T(1024)S(1)} %broadcast_clamp_fusion), kind=kCustom, calls=%fused_computation | custom fusion | bytes 1839104 | tf_op jit(solution)/shard_map/jit(_take)/gather | solution.py:130
  117.6 7.8 %all-to-all-start.2 = ((bf16[32,32,448]{2,1,0:T(8,128)(2,1)}), bf16[32,32,448]{2,1,0:T(8,128)(2,1)S(1)}, u32[]{:S(2)}, u32[]{:S(2)}) async-start(bf16[32,32,448]{2,1,0:T(8,128)(2,1)} %select_select_fusion), calls=%async_computation.2 | async-start | bytes 2097152 | tf_op jit(solution)/shard_map/all_to_all | solution.py:132
  125.7 17.0 %all-to-all-done.2 = bf16[32,32,448]{2,1,0:T(8,128)(2,1)S(1)} async-done(((bf16[32,32,448]{2,1,0:T(8,128)(2,1)}), bf16[32,32,448]{2,1,0:T(8,128)(2,1)S(1)}, u32[]{:S(2)}, u32[]{:S(2)}) %all-to-all-start.2) | async-done | bytes 917536 | tf_op jit(solution)/shard_map/all_to_all | solution.py:132
  145.1 2.4 collective-permute-start.4
  147.5 11.6 %collective-permute-done = bf16[512,448]{1,0:T(8,128)(2,1)S(1)} collective-permute-done((bf16[512,448]{1,0:T(8,128)(2,1)S(1)}, bf16[512,448]{1,0:T(8,128)(2,1)S(1)}, u32[]{:S(2)}, u32[]{:S(2)}) %collective-permute-start) | collective-permute-done | bytes 458784 | tf_op jit(solution)/shard_map/ppermute | solution.py:18
  159.2 2.7 collective-permute-start.5
  161.9 10.7 %collective-permute-done.1 = bf16[512,448]{1,0:T(8,128)(2,1)S(1)} collective-permute-done((bf16[512,448]{1,0:T(8,128)(2,1)S(1)}, bf16[512,448]{1,0:T(8,128)(2,1)S(1)}, u32[]{:S(2)}, u32[]{:S(2)}) %collective-permute-start.1) | collective-permute-done | bytes 458784 | tf_op jit(solution)/shard_map/ppermute | solution.py:18
  172.6 2.7 collective-permute-start.6
  175.3 9.8 %collective-permute-done.2 = bf16[512,448]{1,0:T(8,128)(2,1)S(1)} collective-permute-done((bf16[512,448]{1,0:T(8,128)(2,1)S(1)}, bf16[512,448]{1,0:T(8,128)(2,1)S(1)}, u32[]{:S(2)}, u32[]{:S(2)}) %collective-permute-start.2) | collective-permute-done | bytes 458784 | tf_op jit(solution)/shard_map/ppermute | solution.py:18
  185.1 11.7 %collective-permute-done.3 = bf16[512,448]{1,0:T(8,128)(2,1)} collective-permute-done((bf16[512,448]{1,0:T(8,128)(2,1)S(1)}, bf16[512,448]{1,0:T(8,128)(2,1)}, u32[]{:S(2)}, u32[]{:S(2)}) %collective-permute-start.3) | collective-permute-done | bytes 458784 | tf_op jit(solution)/shard_map/ppermute | solution.py:18
  196.7 11.6 %concatenate.13 = bf16[512,7168]{1,0:T(8,128)(2,1)} concatenate(bf16[512,448]{1,0:T(8,128)(2,1)} %collective-permute-done.3, bf16[512,448]{1,0:T(8,128)(2,1)S(1)} %collective-permute-done.2, bf16[512,448]{1,0:T(8,128)(2,1)S(1)} %collective-permute-done.1, bf16[512,448]{1,0:T(8,128)(2,1)S(1)} %collective-permute-done, bf16[512,448]{1,0:T(8,128)(2,1)S(1)} %broadcast_select_fusion, ...), dimensions={1} | concatenate | bytes 14680064 | tf_op jit(solution)/shard_map/jit(_roll_dynamic)/concatenate | solution.py:22
  208.4 5.2 %fusion.7 = f32[512]{0:T(512)S(1)} fusion(bf16[512,7168]{1,0:T(8,128)(2,1)} %concatenate.13, s32[]{:T(128)S(6)} %select_n.119), kind=kLoop, calls=%fused_computation.11 | loop fusion | flops 5504512 | bytes 3672068 | tf_op jit(solution)/shard_map/reduce_sum | solution.py:68
  213.6 14.2 %fusion.3 = f32[512,1184]{0,1:T(8,128)S(1)} fusion(bf16[3584,3552]{1,0:T(8,128)(2,1)} %all-gather.2.cloned.1.call-done, f32[3584]{0:T(1024)S(1)} %copy-done.7, f32[512]{0:T(512)S(1)} %add_rsqrt_fusion.1, bf16[512,7168]{1,0:T(8,128)(2,1)} %concatenate.13, s32[]{:T(128)S(6)} %select_n.119), kind=kOutput, calls=%fused_computation.5 | convolution fusion | flops 4352638976 | bytes 15286276 | tf_op jit(solution)/shard_map/dot_general | solution.py:151
  227.9 10.2 %fusion.5 = f32[512,1184]{0,1:T(8,128)S(1)} fusion(bf16[3584,3552]{1,0:T(8,128)(2,1)} %all-gather.2.cloned.1.call-done, f32[3584]{0:T(1024)S(1)} %copy-done.7, f32[512]{0:T(512)S(1)} %add_rsqrt_fusion.1, bf16[512,7168]{1,0:T(8,128)(2,1)} %concatenate.13, s32[]{:T(128)S(6)} %select_n.119), kind=kOutput, calls=%fused_computation.7 | convolution fusion | flops 4352638976 | bytes 15286276 | tf_op jit(solution)/shard_map/dot_general | solution.py:150
  238.1 15.8 %fusion.10 = bf16[512,3584]{1,0:T(8,128)(2,1)} fusion(bf16[3584,3552]{1,0:T(8,128)(2,1)} %all-gather.2.cloned.1.call-done, f32[512,1184]{0,1:T(8,128)S(1)} %fusion.3, f32[512,1184]{0,1:T(8,128)S(1)} %fusion.5), kind=kOutput, calls=%fused_computation.14 | convolution fusion | flops 4350771200 | bytes 17694720 | tf_op jit(solution)/shard_map/dot_general | solution.py:153
  253.9 49.2 %reduce-scatter.2.cloned.1.call-done = bf16[64,3584]{1,0:T(8,128)(2,1)} async-done(((bf16[512,3584]{1,0:T(8,128)(2,1)}), bf16[64,3584]{1,0:T(8,128)(2,1)}) %reduce-scatter.2.cloned.1.call-update) | async-done | bytes 458768 | tf_op jit(solution)/shard_map/reduce_scatter | solution.py:154
  303.1 2.2 add_convert_fusion
  (76 shorter events, 19.5 us)
Async XLA Ops:
  6.5 10.3 %copy-start = (bf16[160,1280]{1,0:T(8,128)(2,1)S(1)}, bf16[160,1280]{1,0:T(8,128)(2,1)}, u32[]{:S(2)}) copy-start(bf16[160,1280]{1,0:T(8,128)(2,1)} %param.18) | copy-start | bytes 1228804
  6.5 2.5 copy-start.2
  6.5 2.8 copy-start.5
  6.5 3.1 copy-start.8
  6.5 207.0 %all-gather.2.cloned.1.call-start = ((), (), s32[]{:S(2)}) async-start(), calls=%async_computation.4 | async-start | bytes 26492928 | tf_op jit(solution)/shard_map/all_gather | solution.py:56
  18.5 43.9 %all-to-all-start = ((bf16[8,64,1280]{2,1,0:T(8,128)(2,1)}), bf16[8,64,1280]{2,1,0:T(8,128)(2,1)S(1)}, u32[]{:S(2)}, u32[]{:S(2)}) async-start(bf16[8,64,1280]{2,1,0:T(8,128)(2,1)} %bitcast.15), calls=%async_computation | async-start | bytes 2621440 | tf_op jit(solution)/shard_map/all_to_all | solution.py:32
  62.6 4.9 %copy-start.4 = (s32[32,32]{1,0:T(8,128)S(1)}, s32[32,32]{1,0:T(8,128)}, u32[]{:S(2)}) copy-start(s32[32,32]{1,0:T(8,128)} %param.22) | copy-start | bytes 12292
  62.6 5.5 %copy-start.6 = (f32[1280]{0:T(1024)S(1)}, f32[1280]{0:T(1024)}, u32[]{:S(2)}) copy-start(f32[1280]{0:T(1024)} %param.19) | copy-start | bytes 15364
  62.6 5.5 %copy-start.3 = (bf16[384,448]{0,1:T(8,128)(2,1)S(1)}, bf16[384,448]{0,1:T(8,128)(2,1)}, u32[]{:S(2)}) copy-start(bf16[384,448]{0,1:T(8,128)(2,1)} %param.21) | copy-start | bytes 1032196
  63.9 38.3 %all-to-all-start.1 = ((bf16[8,64,1280]{2,1,0:T(8,128)(2,1)}), bf16[8,64,1280]{2,1,0:T(8,128)(2,1)S(1)}, u32[]{:S(2)}, u32[]{:S(2)}) async-start(bf16[8,64,1280]{2,1,0:T(8,128)(2,1)} %broadcast_in_dim.103), calls=%async_computation.1 | async-start | bytes 2621440 | tf_op jit(solution)/shard_map/all_to_all | solution.py:38
  117.6 25.0 %all-to-all-start.2 = ((bf16[32,32,448]{2,1,0:T(8,128)(2,1)}), bf16[32,32,448]{2,1,0:T(8,128)(2,1)S(1)}, u32[]{:S(2)}, u32[]{:S(2)}) async-start(bf16[32,32,448]{2,1,0:T(8,128)(2,1)} %select_select_fusion), calls=%async_computation.2 | async-start | bytes 2097152 | tf_op jit(solution)/shard_map/all_to_all | solution.py:132
  125.5 177.7 %reduce-scatter.2.cloned.1.call-start = ((), (), s32[]{:S(2)}) async-start(), calls=%async_computation.5 | async-start | bytes 4128768 | tf_op jit(solution)/shard_map/reduce_scatter | solution.py:154
  144.8 14.4 %collective-permute-start = (bf16[512,448]{1,0:T(8,128)(2,1)S(1)}, bf16[512,448]{1,0:T(8,128)(2,1)S(1)}, u32[]{:S(2)}, u32[]{:S(2)}) collective-permute-start(bf16[512,448]{1,0:T(8,128)(2,1)S(1)} %broadcast_select_fusion), channel_id=1, source_target_pairs={{0,1},{1,2},{2,3},{3,4},{4,5},{5,6},{6,7},{7,0},{8,9},{9,10},{10,1... | collective-permute-start | bytes 1376264 | tf_op jit(solution)/shard_map/ppermute | solution.py:18
  145.1 14.0 %collective-permute-start.4 = (bf16[512,448]{1,0:T(8,128)(2,1)S(1)}, bf16[512,448]{1,0:T(8,128)(2,1)S(1)}, u32[]{:S(2)}, u32[]{:S(2)}) collective-permute-start(bf16[512,448]{1,0:T(8,128)(2,1)S(1)} %broadcast_select_fusion), channel_id=1, source_target_pairs={{0,7},{1,0},{2,1},{3,2},{4,3},{5,4},{6,5},{7,6},{8,15},{9,8},{10,9... | collective-permute-start | bytes 1376264 | tf_op jit(solution)/shard_map/ppermute | solution.py:20
  159.2 13.4 %collective-permute-start.1 = (bf16[512,448]{1,0:T(8,128)(2,1)S(1)}, bf16[512,448]{1,0:T(8,128)(2,1)S(1)}, u32[]{:S(2)}, u32[]{:S(2)}) collective-permute-start(bf16[512,448]{1,0:T(8,128)(2,1)S(1)} %collective-permute-done), channel_id=1, source_target_pairs={{0,1},{1,2},{2,3},{3,4},{4,5},{5,6},{6,7},{7,0},{8,9},{9,10},{10,1... | collective-permute-start | bytes 1376264 | tf_op jit(solution)/shard_map/ppermute | solution.py:18
  159.2 13.4 %collective-permute-start.5 = (bf16[512,448]{1,0:T(8,128)(2,1)S(1)}, bf16[512,448]{1,0:T(8,128)(2,1)S(1)}, u32[]{:S(2)}, u32[]{:S(2)}) collective-permute-start(bf16[512,448]{1,0:T(8,128)(2,1)S(1)} %collective-permute-done.4), channel_id=1, source_target_pairs={{0,7},{1,0},{2,1},{3,2},{4,3},{5,4},{6,5},{7,6},{8,15},{9,8},{10,9... | collective-permute-start | bytes 1376264 | tf_op jit(solution)/shard_map/ppermute | solution.py:20
  172.6 12.5 %collective-permute-start.2 = (bf16[512,448]{1,0:T(8,128)(2,1)S(1)}, bf16[512,448]{1,0:T(8,128)(2,1)S(1)}, u32[]{:S(2)}, u32[]{:S(2)}) collective-permute-start(bf16[512,448]{1,0:T(8,128)(2,1)S(1)} %collective-permute-done.1), channel_id=1, source_target_pairs={{0,1},{1,2},{2,3},{3,4},{4,5},{5,6},{6,7},{7,0},{8,9},{9,10},{10,1... | collective-permute-start | bytes 1376264 | tf_op jit(solution)/shard_map/ppermute | solution.py:18
  172.6 12.5 %collective-permute-start.6 = (bf16[512,448]{1,0:T(8,128)(2,1)S(1)}, bf16[512,448]{1,0:T(8,128)(2,1)}, u32[]{:S(2)}, u32[]{:S(2)}) collective-permute-start(bf16[512,448]{1,0:T(8,128)(2,1)S(1)} %collective-permute-done.5), channel_id=1, source_target_pairs={{0,7},{1,0},{2,1},{3,2},{4,3},{5,4},{6,5},{7,6},{8,15},{9,8},{10,9... | collective-permute-start | bytes 1376264 | tf_op jit(solution)/shard_map/ppermute | solution.py:20
  185.1 11.7 %collective-permute-start.3 = (bf16[512,448]{1,0:T(8,128)(2,1)S(1)}, bf16[512,448]{1,0:T(8,128)(2,1)}, u32[]{:S(2)}, u32[]{:S(2)}) collective-permute-start(bf16[512,448]{1,0:T(8,128)(2,1)S(1)} %collective-permute-done.2), channel_id=1, source_target_pairs={{0,1},{1,2},{2,3},{3,4},{4,5},{5,6},{6,7},{7,0},{8,9},{9,10},{10,1... | collective-permute-start | bytes 1376264 | tf_op jit(solution)/shard_map/ppermute | solution.py:18
  208.3 5.3 %copy-start.7 = (f32[3584]{0:T(1024)S(1)}, f32[3584]{0:T(1024)}, u32[]{:S(2)}) copy-start(f32[3584]{0:T(1024)} %param.24) | copy-start | bytes 43012
  238.1 67.3 %copy-start.1 = (bf16[160,1280]{1,0:T(8,128)(2,1)S(1)}, bf16[160,1280]{1,0:T(8,128)(2,1)}, u32[]{:S(2)}) copy-start(bf16[160,1280]{1,0:T(8,128)(2,1)} %param.18) | copy-start | bytes 1228804
Sparse Core Ops, SparseCore 0:
  9.9 102.6 all-gather.1
  254.1 49.0 reduce-scatter.1
